TPU v7x, 256 devices: a whole 4x4x8 slice. The times are simulated.
256 devices in a mesh: depth: 32 (over y, x, core), rows: 8 (over z).
Axes of the slice: x: 4, y: 4, z: 8, core: 2. Of those that a mesh axis runs over, the one named last changes fastest.
Arguments:
- initial: float32 [32, 256, 128], P('rows'), may hold values from -6 to 6
- forward_guess: float32 [64, 32, 256, 128], P('depth', 'rows'), may hold values from -6 to 6
- adjoint_guess: float32 [64, 32, 256, 128], P('depth', 'rows'), may hold values from -6 to 6
- cotangent: float32 [32, 256, 128], P('rows'), may hold values from -6 to 6
- kernel: bfloat16 [3, 3, 128, 128], replicated, may hold values from -0.125 to 0.125
- conv_bias: float32 [128], replicated, may hold values from -1.5 to 1.5
Outputs:
- states: float32 [64, 32, 256, 128], P('depth', 'rows')
- adjoints: float32 [64, 32, 256, 128], P('depth', 'rows')
- grad_kernel: float32 [3, 3, 128, 128], replicated
- grad_bias: float32 [128], replicated
All inputs are finite; a program needn't handle non-finite values.
Results may differ from a plain program's by a relative error of at most 0.0025.
The roundings to bfloat16 on the way count: a program that leaves them out, or rounds other values in their place, can miss the bound.
Values may be sent and summed in bfloat16 or wider, within the bound.
No kernel may reach another device: no remote copies, remote signals or barrier semaphores. Data moves between devices by JAX's collectives and lax.ppermute only.
A program may use at most 64 MiB of HBM per device.

v0:
```python
import jax
import jax.numpy as jnp
from jax import lax
from jax.sharding import PartitionSpec as P

STEP_SIZE = 0.2


def padded_2(shard, sides, width):
    for axis, dim in sides:
        devices, length = (lax.axis_size(axis), shard.shape[dim])
        up = [(i, (i + 1) % devices) for i in range(devices - 1)]
        down = [(j, i) for i, j in up]
        last = lax.slice_in_dim(shard, length - width, length, axis=dim)
        leading = lax.slice_in_dim(shard, 0, width, axis=dim)
        before = lax.ppermute(last, axis, up)
        after = lax.ppermute(leading, axis, down)
        shard = jnp.concatenate([before, shard, after], axis=dim)
    return shard


def passed_along(value, axis, steps):
    count = lax.axis_size(axis)
    leading, last = (max(0, -steps), min(count, count - steps))
    return lax.ppermute(value, axis, [(source, source + steps) for source in range(leading, last)])


def restrict(signal):
    row_count, col_count, channels = signal.shape
    return signal.reshape(row_count // 2, 2, col_count // 2, 2, channels).mean(axis=(1, 3))


def prolong(signal):
    return jnp.repeat(jnp.repeat(signal, 2, axis=0), 2, axis=1)


def taps_product(padded, kernel, row_count, col_count):
    summed = jnp.zeros((row_count * col_count, kernel.shape[3]), jnp.float32)
    for row_tap in range(3):
        for col_tap in range(3):
            window = padded[row_tap : row_tap + row_count, col_tap : col_tap + col_count].reshape(
                row_count * col_count, -1
            )
            summed = summed + jnp.dot(
                window, kernel[row_tap, col_tap], preferred_element_type=jnp.float32
            )
    return summed.reshape(row_count, col_count, -1)


def surround(signal, on_coarse):
    if on_coarse:
        padded = padded_2(signal, (("rows", 0),), 1)
    else:
        padded = padded_2(signal, (("rows", 0),), 1)
    return jnp.pad(padded, ((0, 0), (1, 1), (0, 0)))


def advance(current, kernel, conv_bias, on_coarse):
    factor = 2.0 * STEP_SIZE if on_coarse else STEP_SIZE
    squashed = jnp.tanh(current).astype(jnp.bfloat16)
    padded = surround(squashed, on_coarse)
    return current + factor * (
        taps_product(padded, kernel, current.shape[0], current.shape[1]) + conv_bias
    )


def retreat(current, adjoint, kernel_flip, on_coarse):
    factor = 2.0 * STEP_SIZE if on_coarse else STEP_SIZE
    derivative = 1.0 - jnp.tanh(current) ** 2
    padded = surround(adjoint.astype(jnp.bfloat16), on_coarse)
    return adjoint + factor * derivative * taps_product(
        padded, kernel_flip, adjoint.shape[0], adjoint.shape[1]
    )


def kernel_terms(padded, cotan, row_count, col_count):
    flat = cotan.reshape(row_count * col_count, -1)
    tap_rows = []
    for row_tap in range(3):
        tap_cols = []
        for col_tap in range(3):
            window = padded[row_tap : row_tap + row_count, col_tap : col_tap + col_count].reshape(
                row_count * col_count, -1
            )
            tap_cols.append(
                lax.dot_general(
                    window, flat, (((0,), (0,)), ((), ())), preferred_element_type=jnp.float32
                )
            )
        tap_rows.append(jnp.stack(tap_cols))
    return jnp.stack(tap_rows)


def shards(initial, forward_guess, adjoint_guess, cotangent, kernel, conv_bias):
    block_count = lax.axis_size("depth")
    depth_pos = lax.axis_index("depth")
    at_first = depth_pos == 0
    at_last = depth_pos == block_count - 1
    row_count, col_count = (initial.shape[0], initial.shape[1])
    kernel_flip = jnp.transpose(jnp.flip(kernel, (0, 1)), (0, 1, 3, 2))
    coarse_start = restrict(initial)
    guess_point = forward_guess[1]
    previous = passed_along(guess_point, "depth", 1)
    previous = jnp.where(at_first, initial, previous)
    relaxed_odd = advance(previous, kernel, conv_bias, False)
    rhs_local = restrict(advance(relaxed_odd, kernel, conv_bias, False)) - advance(
        restrict(previous), kernel, conv_bias, True
    )

    def forward_turn(step_no, state_pair):
        incoming, kept_state = state_pair
        result = advance(incoming, kernel, conv_bias, True) + rhs_local
        kept_state = jnp.where(step_no == depth_pos, result, kept_state)
        incoming = passed_along(result, "depth", 1)
        return (incoming, kept_state)

    last_coarse, stored = lax.fori_loop(
        0, block_count, forward_turn, (coarse_start, jnp.zeros_like(coarse_start))
    )
    corrected = guess_point + prolong(stored - restrict(guess_point))
    prev_fixed, prev_coarse = passed_along((corrected, stored), "depth", 1)
    prev_fixed = jnp.where(at_first, initial, prev_fixed)
    linear = jnp.where(at_first, coarse_start, prev_coarse)
    state_odd = advance(prev_fixed, kernel, conv_bias, False)
    guess_even = adjoint_guess[0]
    ahead = passed_along(guess_even, "depth", -1)
    ahead = jnp.where(at_last, cotangent, ahead)
    relaxed_adj = retreat(state_odd, ahead, kernel_flip, False)
    residual = retreat(prev_fixed, relaxed_adj, kernel_flip, False) - guess_even
    coarse_res = restrict(residual)

    def backward_turn(step_no, state_pair):
        incoming, kept_error = state_pair
        result = retreat(linear, incoming, kernel_flip, True) + coarse_res
        kept_error = jnp.where(step_no == block_count - 1 - depth_pos, result, kept_error)
        incoming = passed_along(result, "depth", -1)
        return (incoming, kept_error)

    final_error, error_own = lax.fori_loop(
        0, block_count, backward_turn, (jnp.zeros_like(coarse_start), jnp.zeros_like(coarse_start))
    )
    corrected_adj = guess_even + prolong(error_own)
    ahead_fixed = passed_along(corrected_adj, "depth", -1)
    ahead_fixed = jnp.where(at_last, cotangent, ahead_fixed)
    adjoint_odd = retreat(state_odd, ahead_fixed, kernel_flip, False)
    squashed_even = surround(jnp.tanh(prev_fixed).astype(jnp.bfloat16), False)
    squashed_odd = surround(jnp.tanh(state_odd).astype(jnp.bfloat16), False)
    local_grad = kernel_terms(squashed_even, adjoint_odd.astype(jnp.bfloat16), row_count, col_count)
    local_grad = local_grad + kernel_terms(
        squashed_odd, ahead_fixed.astype(jnp.bfloat16), row_count, col_count
    )
    local_bias = jnp.sum(adjoint_odd, axis=(0, 1)) + jnp.sum(ahead_fixed, axis=(0, 1))
    grad_sum, bias_sum = lax.psum((local_grad, local_bias), ("depth", "rows"))
    factor = STEP_SIZE / (row_count * lax.axis_size("rows") * col_count)
    states_out = jnp.stack([state_odd, corrected])
    adjoints_out = jnp.stack([corrected_adj, adjoint_odd])
    return (states_out, adjoints_out, grad_sum * factor, bias_sum * factor)


def solution(mesh):
    placed = (
        P("rows", None, None),
        P("depth", "rows", None, None),
        P("depth", "rows", None, None),
        P("rows", None, None),
        P(),
        P(),
    )
    return jax.shard_map(
        shards,
        mesh=mesh,
        in_specs=placed,
        out_specs=(P("depth", "rows", None, None), P("depth", "rows", None, None), P(), P()),
        check_vma=False,
    )
```

profile of v0, /device:TPU:1, one launch (start us, length us, event | category | flops | bytes accessed | tf_op | source)
XLA Modules:
  0.0 1818.0 jit_solution(15526250043578704130)
XLA Ops:
  127.0 579.7 %while.36 = (s32[]{:T(128)}, f32[2,128,128]{2,1,0:T(8,128)S(1)}, f32[2,128,128]{2,1,0:T(8,128)S(1)}, bf16[3,3,128,128]{3,2,1,0:T(8,128)(2,1)S(1)}, f32[128]{0:T(...) while((s32[]{:T(128)}, f32[2,128,128]{2,1,0:T(8,128)S(1)}, ...), condition=%wide.region_4.5_spmd.clone, body=%wide.region_3.4_spmd.clone.sunk | while | flops 76853248 | bytes 6327017 | solution.py:117
  355.8 7.6 collective-permute-start.2
  374.8 7.6 collective-permute-start.2
  393.7 7.6 collective-permute-start.2
  412.7 7.6 collective-permute-start.2
  431.7 7.6 collective-permute-start.2
  450.6 7.6 collective-permute-start.2
  469.6 7.6 collective-permute-start.2
  488.5 7.6 collective-permute-start.2
  507.5 7.6 collective-permute-start.2
  526.5 7.6 collective-permute-start.2
  545.4 7.6 collective-permute-start.2
  564.4 7.6 collective-permute-start.2
  583.4 7.6 collective-permute-start.2
  602.3 7.6 collective-permute-start.2
  621.3 7.6 collective-permute-start.2
  640.3 7.6 collective-permute-start.2
  678.2 7.6 collective-permute-start.2
  810.8 659.7 %while.37 = (s32[]{:T(128)}, f32[2,128,128]{2,1,0:T(8,128)S(1)}, f32[2,128,128]{2,1,0:T(8,128)S(1)}, f32[2,128,128]{2,1,0:T(8,128)S(1)}, bf16[3,3,128,128]{3,2,1...) while((s32[]{:T(128)}, f32[2,128,128]{2,1,0:T(8,128)S(1)}, ...), condition=%wide.region_8.9_spmd.clone, body=%wide.region_7.8_spmd.clone.sunk | while | flops 76886016 | bytes 7244093 | solution.py:139
  824.9 10.2 collective-permute-done.5
  868.0 10.2 collective-permute-done.5
  911.1 10.8 collective-permute-done.5
  1531.3 105.2 %psum.15 = f32[128]{0:T(128)S(1)} all-reduce(f32[128]{0:T(128)S(1)} %add.599), channel_id=1, replica_groups=mesh['depth'=32,'rows'=8] {'depth','rows'}, use_global_device_ids=true, to_apply=%region_12.13 | all-reduce | flops 128 | bytes 1024 | tf_op jit(solution)/shard_map/psum | solution.py:153
  1637.0 172.2 %all-reduce.12.cloned.1.call-done = f32[3,3,128,128]{3,2,1,0:T(8,128)} async-done(((f32[3,3,128,128]{3,2,1,0:T(8,128)}), f32[3,3,128,128]{3,2,1,0:T(8,128)}) %all-reduce.12.cloned.1.call-update) | async-done | bytes 589840 | tf_op jit(solution)/shard_map/psum | solution.py:153
  (1960 shorter events, 1355.9 us)
Async XLA Ops:
  7.2 1802.1 %all-reduce.12.cloned.1.call-start = ((), (), s32[]{:S(2)}) async-start(), calls=%async_computation | async-start | bytes 1179648 | tf_op jit(solution)/shard_map/psum | solution.py:153
  8.4 13.3 collective-permute-start.17
  27.8 16.5 collective-permute-start.11
  31.3 14.3 collective-permute-start.12
  35.0 14.3 collective-permute-start.18
  39.0 10.3 collective-permute-start.19
  40.3 19.8 %collective-permute-start.7 = (bf16[1,256,128]{1,2,0:T(8,128)(2,1)}, bf16[1,256,128]{1,2,0:T(8,128)(2,1)S(1)}, u32[]{:S(2)}, u32[]{:S(2)}) collective-permute-start(bf16[1,256,128]{1,2,0:T(8,128)(2,1)} %get-tuple-element.543), channel_id=1, source_target_pairs={{0,1},{1,2},{2,3},{3,4},{4,5},{5,6},{6,7},{8,9},{9,10},{10,11},{11... | collective-permute-start | bytes 196616 | tf_op jit(solution)/shard_map/ppermute | solution.py:16
  44.3 15.8 collective-permute-start.8
  85.2 13.3 collective-permute-start.10
  86.5 12.0 collective-permute-start.9
  355.8 9.5 collective-permute-start.2
  393.7 9.5 collective-permute-start.2
  412.7 9.5 collective-permute-start.2
  708.0 13.0 collective-permute-start.13
  723.7 16.0 collective-permute-start.14
  728.8 10.8 collective-permute-start.15
  731.3 42.4 %collective-permute-start.16 = (f32[2,128,128]{2,1,0:T(8,128)S(1)}, f32[2,128,128]{2,1,0:T(8,128)}, u32[]{:S(2)}, u32[]{:S(2)}) collective-permute-start(f32[2,128,128]{2,1,0:T(8,128)S(1)} %get-tuple-element.361), channel_id=1, source_target_pairs={{0,8},{8,16},{16,24},{24,32},{32,40},{40,48},{48,56},{56,64},{64,7... | collective-permute-start | bytes 393224 | tf_op jit(solution)/shard_map/ppermute | solution.py:25
  765.8 9.7 collective-permute-start.20
  823.0 12.2 collective-permute-start.5
  866.0 12.1 collective-permute-start.5
  909.1 12.7 collective-permute-start.5
  1475.5 18.2 %collective-permute-start.22 = (f32[4,256,128]{1,2,0:T(8,128)}, f32[4,256,128]{1,2,0:T(8,128)}, u32[]{:S(2)}, u32[]{:S(2)}) collective-permute-start(f32[4,256,128]{1,2,0:T(8,128)} %bitcast_add_fusion), channel_id=1, source_target_pairs={{8,0},{16,8},{24,16},{32,24},{40,32},{48,40},{56,48},{64,56},{72,6... | collective-permute-start | bytes 1572872 | tf_op jit(solution)/shard_map/ppermute | solution.py:25
  1480.7 12.7 collective-permute-start.25
  1498.4 9.9 collective-permute-start.23
  (370 other events, 2269.7 us)
Sparse Core Ops, SparseCore 0:
  1529.7 279.5 all-reduce.11
where the time goes:
time: 1830 us; the launch traced here: 1820 us
  starting transfers between devices  785 us (43%)
  waiting for transfers between devices  524 us (29%)
  local copies, waits for them, and re-layouts  184 us (10%)
  matrix products  117 us (6%)
  blocking collectives  105 us (6%)
  other arithmetic  78.5 us (4%)
    ppermute x72, starting transfers between devices, padded_2(): before = lax.ppermute(last, axis, up)  393 us
    ppermute x69, starting transfers between devices, passed_along(): lax.ppermute(value, axis, [(source, source + steps) for source in range(l...  299 us
    ppermute x69, waiting for transfers between devices, passed_along(): lax.ppermute(value, axis, [(source, source + steps) for source in range(l...  283 us
    psum x1, waiting for transfers between devices, shards(): grad_sum, bias_sum = lax.psum((local_grad, local_bias), ('depth', 'rows'))  172 us
    dot_general x639, matrix products, taps_product(): jnp.dot(window, kernel[row_tap, col_tap], preferred_element_type=jnp.floa...  113 us
    psum x1, blocking collectives, shards(): grad_sum, bias_sum = lax.psum((local_grad, local_bias), ('depth', 'rows'))  105 us
    ppermute x72, starting transfers between devices, padded_2(): after = lax.ppermute(leading, axis, down)  93.1 us
    slice x119, local copies, waits for them, and re-layouts, taps_product(): padded[row_tap:row_tap + row_count, col_tap:col_tap + col_count]  79.3 us
  transfers between devices with their start and end apart: 214, of which 132 were waited for; matrix products, arithmetic and copies ran while one was open for 4% of the time, Pallas kernels for 0%

commit v1 on v0

--- a/solution.py
+++ b/solution.py
@@ -150,7 +150,7 @@
         squashed_odd, ahead_fixed.astype(jnp.bfloat16), row_count, col_count
     )
     local_bias = jnp.sum(adjoint_odd, axis=(0, 1)) + jnp.sum(ahead_fixed, axis=(0, 1))
-    grad_sum, bias_sum = lax.psum((local_grad, local_bias), ("depth", "rows"))
+    grad_sum, bias_sum = jax.lax.psum(jax.lax.psum((local_grad, local_bias), "rows"), "depth")
     factor = STEP_SIZE / (row_count * lax.axis_size("rows") * col_count)
     states_out = jnp.stack([state_odd, corrected])
     adjoints_out = jnp.stack([corrected_adj, adjoint_odd])

time: 1830 us -> 1670 us (0.913)
  local copies, waits for them, and re-layouts: 184 us -> 125 us
  waiting for transfers between devices: 524 us -> 473 us
  other arithmetic: 78.5 us -> 55.6 us
  blocking collectives: 105 us -> 83.6 us
    psum x1 -> x2, waiting for transfers between devices: 172 us -> 120 us  [the longest x1 86.2 us: shards(): jax.lax.psum((local_grad, local_bias), 'rows')]
    while x192 -> x0, local copies, waits for them, and re-layouts: 36.7 us -> none
    psum x1 -> x2, blocking collectives: 105 us -> 83.6 us  [the longest x1 71.1 us: shards(): jax.lax.psum(jax.lax.psum((local_grad, local_bias), 'rows'), 'depth')]
    select_n x32, other arithmetic: 23.5 us -> 3.13 us  [backward_turn(): jnp.where(step_no == block_count - 1 - depth_pos, result, kept_error)]
    slice x72, local copies, waits for them, and re-layouts: 24.1 us -> 4.45 us  [padded_2(): last = lax.slice_in_dim(shard, length - width, length, axis=dim)]
  transfers between devices with their start and end apart: 214 -> 215, of which waited for: 132 -> 134; matrix products, arithmetic and copies ran while one was open for 4% -> 4% of each run, Pallas kernels for 0% -> 0%
where the time goes in v1:
time: 1670 us; the launch traced here: 1660 us
  starting transfers between devices  784 us (47%)
  waiting for transfers between devices  473 us (28%)
  local copies, waits for them, and re-layouts  125 us (7%)
  matrix products  117 us (7%)
  blocking collectives  83.6 us (5%)
  other arithmetic  55.6 us (3%)
    ppermute x72, starting transfers between devices, padded_2(): before = lax.ppermute(last, axis, up)  393 us
    ppermute x69, starting transfers between devices, passed_along(): lax.ppermute(value, axis, [(source, source + steps) for source in range(l...  298 us
    ppermute x69, waiting for transfers between devices, passed_along(): lax.ppermute(value, axis, [(source, source + steps) for source in range(l...  278 us
    dot_general x639, matrix products, taps_product(): jnp.dot(window, kernel[row_tap, col_tap], preferred_element_type=jnp.floa...  112 us
    ppermute x72, starting transfers between devices, padded_2(): after = lax.ppermute(leading, axis, down)  93.2 us
    psum x1, waiting for transfers between devices, shards(): jax.lax.psum((local_grad, local_bias), 'rows')  86.2 us
    slice x119, local copies, waits for them, and re-layouts, taps_product(): padded[row_tap:row_tap + row_count, col_tap:col_tap + col_count]  79.3 us
    psum x1, blocking collectives, shards(): jax.lax.psum(jax.lax.psum((local_grad, local_bias), 'rows'), 'depth')  71.1 us
  transfers between devices with their start and end apart: 215, of which 134 were waited for; matrix products, arithmetic and copies ran while one was open for 4% of the time, Pallas kernels for 0%

profile of v1, /device:TPU:1, one launch (start us, length us, event | category | flops | bytes accessed | tf_op | source)
XLA Modules:
  0.0 1662.5 jit_solution(18264620251514977755)
XLA Ops:
  128.3 579.6 %while.36 = (s32[]{:T(128)}, f32[2,128,128]{2,1,0:T(8,128)S(1)}, f32[2,128,128]{2,1,0:T(8,128)S(1)}, bf16[3,3,128,128]{3,2,1,0:T(8,128)(2,1)S(1)}, f32[128]{0:T(...) while((s32[]{:T(128)}, f32[2,128,128]{2,1,0:T(8,128)S(1)}, ...), condition=%wide.region_4.5_spmd.clone, body=%wide.region_3.4_spmd.clone.sunk | while | flops 76853248 | bytes 6327017 | solution.py:117
  357.1 7.6 collective-permute-start.2
  376.0 7.6 collective-permute-start.2
  395.0 7.6 collective-permute-start.2
  414.0 7.6 collective-permute-start.2
  432.9 7.6 collective-permute-start.2
  451.9 7.6 collective-permute-start.2
  470.8 7.6 collective-permute-start.2
  489.8 7.6 collective-permute-start.2
  508.8 7.6 collective-permute-start.2
  527.7 7.6 collective-permute-start.2
  546.7 7.6 collective-permute-start.2
  565.7 7.6 collective-permute-start.2
  584.6 7.6 collective-permute-start.2
  641.5 7.6 collective-permute-start.2
  679.5 7.6 collective-permute-start.2
  810.0 578.3 %while.37 = (s32[]{:T(128)}, f32[2,128,128]{2,1,0:T(8,128)S(1)}, f32[2,128,128]{2,1,0:T(8,128)S(1)}, f32[2,128,128]{2,1,0:T(8,128)S(1)}, bf16[3,3,128,128]{3,2,1...) while((s32[]{:T(128)}, f32[2,128,128]{2,1,0:T(8,128)S(1)}, ...), condition=%wide.region_8.9_spmd.clone, body=%wide.region_7.8_spmd.clone.sunk | while | flops 76886016 | bytes 6457577 | solution.py:139
  821.7 11.0 collective-permute-done.5
  859.6 11.0 collective-permute-done.5
  898.0 11.2 collective-permute-done.5
  1447.9 86.2 %all-reduce.13.cloned.1.call-done = f32[3,3,128,128]{3,2,1,0:T(8,128)} async-done(((f32[3,3,128,128]{3,2,1,0:T(8,128)}), f32[3,3,128,128]{3,2,1,0:T(8,128)}) %all-reduce.13.cloned.1.call-update) | async-done | bytes 589840 | tf_op jit(solution)/shard_map/psum | solution.py:153
  1535.6 12.5 psum.30
  1548.1 71.1 %psum.31 = f32[128]{0:T(128)S(1)} all-reduce(f32[128]{0:T(128)S(1)} %psum.30), channel_id=1, replica_groups=mesh['depth'=32,'rows'=8] {'depth'}, use_global_device_ids=true, to_apply=%region_14.15 | all-reduce | flops 128 | bytes 1024 | tf_op jit(solution)/shard_map/psum | solution.py:153
  1619.7 34.0 %all-reduce.15.cloned.1.call-done = f32[3,3,128,128]{3,2,1,0:T(8,128)} async-done(((f32[3,3,128,128]{3,2,1,0:T(8,128)}), f32[3,3,128,128]{3,2,1,0:T(8,128)}) %all-reduce.15.cloned.1.call-update) | async-done | bytes 589840 | tf_op jit(solution)/shard_map/psum | solution.py:153
  (1772 shorter events, 1287.8 us)
Async XLA Ops:
  7.2 1527.0 %all-reduce.13.cloned.1.call-start = ((), (), s32[]{:S(2)}) async-start(), calls=%async_computation | async-start | bytes 1179648 | tf_op jit(solution)/shard_map/psum | solution.py:153
  8.4 13.3 collective-permute-start.17
  27.8 16.5 collective-permute-start.11
  31.3 14.2 collective-permute-start.12
  35.0 14.3 collective-permute-start.18
  39.0 10.3 collective-permute-start.19
  40.3 20.0 %collective-permute-start.7 = (bf16[1,256,128]{1,2,0:T(8,128)(2,1)}, bf16[1,256,128]{1,2,0:T(8,128)(2,1)S(1)}, u32[]{:S(2)}, u32[]{:S(2)}) collective-permute-start(bf16[1,256,128]{1,2,0:T(8,128)(2,1)} %get-tuple-element.543), channel_id=1, source_target_pairs={{0,1},{1,2},{2,3},{3,4},{4,5},{5,6},{6,7},{8,9},{9,10},{10,11},{11... | collective-permute-start | bytes 196616 | tf_op jit(solution)/shard_map/ppermute | solution.py:16
  44.3 16.0 collective-permute-start.8
  85.2 13.3 collective-permute-start.10
  86.5 12.0 collective-permute-start.9
  357.1 9.5 collective-permute-start.2
  395.0 9.5 collective-permute-start.2
  432.9 9.5 collective-permute-start.2
  470.8 9.5 collective-permute-start.2
  489.8 9.5 collective-permute-start.2
  709.3 13.0 collective-permute-start.13
  724.2 15.6 collective-permute-start.14
  730.0 9.8 collective-permute-start.15
  732.5 42.2 %collective-permute-start.16 = (f32[2,128,128]{2,1,0:T(8,128)S(1)}, f32[2,128,128]{2,1,0:T(8,128)}, u32[]{:S(2)}, u32[]{:S(2)}) collective-permute-start(f32[2,128,128]{2,1,0:T(8,128)S(1)} %get-tuple-element.361), channel_id=1, source_target_pairs={{0,8},{8,16},{16,24},{24,32},{32,40},{40,48},{48,56},{56,64},{64,7... | collective-permute-start | bytes 393224 | tf_op jit(solution)/shard_map/ppermute | solution.py:25
  819.8 12.9 collective-permute-start.5
  857.7 12.9 collective-permute-start.5
  896.0 13.1 collective-permute-start.5
  1390.7 14.2 collective-permute-start.22
  1441.6 212.2 %all-reduce.15.cloned.1.call-start = ((), (), s32[]{:S(2)}) async-start(), calls=%async_computation.1 | async-start | bytes 1179648 | tf_op jit(solution)/shard_map/psum | solution.py:153
  (275 other events, 2879.5 us)
Sparse Core Ops, SparseCore 0:
  1441.7 92.4 all-reduce.12
  1537.4 116.2 all-reduce.14
